TPU v7x, 256 devices: a whole 4x4x8 slice. The times are simulated.
256 devices in a mesh: dp: 32 (over x, y, core), etp: 8 (over z).
Axes of the slice: x: 4, y: 4, z: 8, core: 2. Of those that a mesh axis runs over, the one named last changes fastest.
Arguments:
- tokens: bfloat16 [8192, 3072], P('dp'), may hold values from -6 to 6
- cotangent: bfloat16 [8192, 3072], P('dp'), may hold values from -6 to 6
- w_gate: float32 [2, 3072, 6144], P(None, 'dp', 'etp'), may hold values from -0.109375 to 0.109375
- w_up: float32 [2, 3072, 6144], P(None, 'dp', 'etp'), may hold values from -0.109375 to 0.109375
- w_down: float32 [2, 6144, 3072], P(None, 'etp', 'dp'), may hold values from -0.078125 to 0.078125
- slot_token: int32 [16384], P('dp'), may hold values from 0 to 255, as said below
- slot_gate: int32 [16384], P('dp'), may hold values from 0 to 16
- block_expert: int32 [128], P('dp'), may hold values from 0 to 2, as said below
Outputs:
- combined: bfloat16 [8192, 3072], P('dp', 'etp')
- input_grad: bfloat16 [8192, 3072], P('dp', 'etp')
Inputs may be any that keep to these rules, and one draw needn't show every extreme that they name: `slot_token`: within the live blocks of one expert on one dp index no token repeats, so each expert has at most 2 live blocks there. `block_expert`: blocks of the experts and padding blocks stand in any order; each expert has at most 2 blocks on one dp index, and on some dp index every block is live.
All inputs are finite; a program needn't handle non-finite values.
Results may differ from a plain program's by a relative error of at most 0.014.
Values may be sent and summed in bfloat16 or wider, within the bound.
A program may use at most 128 MiB of HBM per device.

v0:
```python
import jax
import jax.numpy as jnp
from jax import lax
from jax.sharding import PartitionSpec as P

gate_steps = 16.0


def block_terms(
    gate_mat,
    up_mat,
    down_mat,
    tokens,
    cotangent,
    slot_token,
    scale,
    block_index,
    block_rows,
    totals,
):
    y_total, dx_total = totals
    row_start = block_index * block_rows
    token_rows = lax.dynamic_slice_in_dim(slot_token, row_start, block_rows, 0)
    gate_scale = lax.dynamic_slice_in_dim(scale, row_start, block_rows, 0)[:, None]
    inputs = tokens[token_rows]
    upstream = cotangent[token_rows]
    gate_pre = jnp.dot(inputs, gate_mat, preferred_element_type=jnp.float32)
    up_pre = jnp.dot(inputs, up_mat, preferred_element_type=jnp.float32)
    squash = jax.nn.sigmoid(gate_pre)
    active = gate_pre * squash
    hidden = (active * up_pre).astype(jnp.bfloat16)
    produced = jnp.dot(hidden, down_mat, preferred_element_type=jnp.float32) * gate_scale
    d_out = (gate_scale * upstream.astype(jnp.float32)).astype(jnp.bfloat16)
    contract_last = (((1,), (1,)), ((), ()))
    d_hidden = lax.dot_general(d_out, down_mat, contract_last, preferred_element_type=jnp.float32)
    d_pre = (d_hidden * up_pre * squash * (1.0 + gate_pre * (1.0 - squash))).astype(jnp.bfloat16)
    d_up = (d_hidden * active).astype(jnp.bfloat16)
    backward = lax.dot_general(d_pre, gate_mat, contract_last, preferred_element_type=jnp.float32)
    backward = backward + lax.dot_general(
        d_up, up_mat, contract_last, preferred_element_type=jnp.float32
    )
    return (y_total.at[token_rows].add(produced), dx_total.at[token_rows].add(backward))


def shards(tokens, cotangent, w_gate, w_up, w_down, slot_token, slot_gate, block_expert):
    experts_count = w_gate.shape[0]
    block_count = block_expert.shape[0]
    block_rows = slot_token.shape[0] // block_count
    scale = slot_gate.astype(jnp.float32) / gate_steps
    gate_low = w_gate.astype(jnp.bfloat16)
    up_low = w_up.astype(jnp.bfloat16)
    down_low = w_down.astype(jnp.bfloat16)
    zeroed = jnp.zeros(tokens.shape, jnp.float32)
    totals = (zeroed, zeroed)

    def skip_block(state):
        return state

    gate_all, up_all = (
        lax.all_gather(gate_low, "dp", axis=1, tiled=True),
        lax.all_gather(up_low, "dp", axis=1, tiled=True),
    )
    down_all = lax.all_gather(down_low, "dp", axis=2, tiled=True)

    def visit_all(block_index, state):
        expert = block_expert[block_index]
        chosen = jnp.minimum(expert, experts_count - 1)

        def compute_block(inner):
            gate_mat = lax.dynamic_index_in_dim(gate_all, chosen, 0, keepdims=False)
            up_mat = lax.dynamic_index_in_dim(up_all, chosen, 0, keepdims=False)
            down_mat = lax.dynamic_index_in_dim(down_all, chosen, 0, keepdims=False)
            return block_terms(
                gate_mat,
                up_mat,
                down_mat,
                tokens,
                cotangent,
                slot_token,
                scale,
                block_index,
                block_rows,
                inner,
            )

        return lax.cond(expert < experts_count, compute_block, skip_block, state)

    totals = lax.fori_loop(0, block_count, visit_all, totals)
    combined, input_grad = (
        lax.psum_scatter(
            totals[0].astype(jnp.bfloat16), "etp", scatter_dimension=1, tiled=True
        ).astype(jnp.float32),
        lax.psum_scatter(
            totals[1].astype(jnp.bfloat16), "etp", scatter_dimension=1, tiled=True
        ).astype(jnp.float32),
    )
    return (combined.astype(jnp.bfloat16), input_grad.astype(jnp.bfloat16))


def solution(mesh):
    in_specs = (
        P("dp", None),
        P("dp", None),
        P(None, "dp", "etp"),
        P(None, "dp", "etp"),
        P(None, "etp", "dp"),
        P("dp"),
        P("dp"),
        P("dp"),
    )
    out_specs = (P("dp", "etp"), P("dp", "etp"))
    return jax.shard_map(shards, mesh=mesh, in_specs=in_specs, out_specs=out_specs, check_vma=False)
```

profile of v0, /device:TPU:4, one launch (start us, length us, event | category | flops | bytes accessed | tf_op | source)
XLA Modules:
  0.0 489.0 jit_solution(1903295765239692804)
XLA Ops:
  7.2 2.2 copy.18
  9.5 0.0 all-gather.4.cloned.1.call-start
  9.5 1.8 convert_element_type.44
  11.4 0.0 all-gather.6.cloned.1.call-start
  11.4 1.8 convert_element_type.45
  13.3 60.4 %all-gather.8.cloned.1.call-done = bf16[2,768,3072]{1,0,2:T(2,128)(2,1)} async-done(((bf16[2,768,96]{1,0,2:T(2,128)(2,1)}), bf16[2,768,3072]{1,0,2:T(2,128)(2,1)}) %all-gather.8.cloned.1.call-update) | async-done | bytes 9437200 | tf_op jit(solution)/shard_map/all_gather | solution.py:63
  73.7 23.8 %copy.12 = bf16[2,768,3072]{2,1,0:T(8,128)(2,1)} copy(bf16[2,768,3072]{1,0,2:T(2,128)(2,1)} %all-gather.8.cloned.1.call-done) | data formatting | bytes 18874368 | tf_op jit(solution)/shard_map/while | solution.py:88
  97.5 38.7 %all-gather.4.cloned.1.call-done = bf16[2,3072,768]{2,1,0:T(8,128)(2,1)} async-done(((bf16[2,96,768]{2,1,0:T(8,128)(2,1)}), bf16[2,3072,768]{2,1,0:T(8,128)(2,1)}) %all-gather.4.cloned.1.call-update) | async-done | bytes 9437200 | tf_op jit(solution)/shard_map/all_gather | solution.py:60
  136.2 62.5 %all-gather.6.cloned.1.call-done = bf16[2,3072,768]{2,1,0:T(8,128)(2,1)} async-done(((bf16[2,96,768]{2,1,0:T(8,128)(2,1)}), bf16[2,3072,768]{2,1,0:T(8,128)(2,1)}) %all-gather.6.cloned.1.call-update) | async-done | bytes 9437200 | tf_op jit(solution)/shard_map/all_gather | solution.py:61
  198.7 0.3 broadcast_in_dim.4
  199.0 2.1 broadcast_in_dim.4.clone
  201.1 5.1 %while.15 = (s32[]{:T(128)}, f32[256,3072]{1,0:T(8,128)S(1)}, f32[256,3072]{1,0:T(8,128)}, s32[4]{0:T(128)S(1)}, s32[512]{0:T(512)}, /*index=5*/bf16[256,3072]{1...) while((s32[]{:T(128)}, f32[256,3072]{1,0:T(8,128)S(1)}, ...), condition=%wide.region_5.6_spmd, body=%wide.region_0.5_spmd.sunk | while | flops 3628795392 | bytes 59779048 | solution.py:88
  201.1 0.6 dynamic_slice.54
  202.4 0.6 dynamic_slice.54
  203.7 0.6 dynamic_slice.54
  204.9 0.6 dynamic_slice.54
  206.2 1.4 convert_element_type.48
  207.6 2.8 copy.13
  210.4 1.4 convert_element_type.49
  211.8 2.6 copy.15
  214.4 224.6 %reduce-scatter.7.cloned.1.call-done = bf16[384,256]{1,0:T(8,128)(2,1)} async-done(((bf16[3072,256]{1,0:T(8,128)(2,1)}), bf16[384,256]{1,0:T(8,128)(2,1)}) %reduce-scatter.7.cloned.1.call-update) | async-done | bytes 196624
  439.0 1.7 copy.14
  440.8 40.0 %reduce-scatter.9.cloned.1.call-done = bf16[384,256]{1,0:T(8,128)(2,1)} async-done(((bf16[3072,256]{1,0:T(8,128)(2,1)}), bf16[384,256]{1,0:T(8,128)(2,1)}) %reduce-scatter.9.cloned.1.call-update) | async-done | bytes 196624
  480.8 1.7 copy.16
  (19 shorter events, 0.3 us)
Async XLA Ops:
  7.2 6.1 %copy-start.4 = (s32[512]{0:T(512)S(1)}, s32[512]{0:T(512)}, u32[]{:S(2)}) copy-start(s32[512]{0:T(512)} %param.18) | copy-start | bytes 6148
  7.2 66.5 %all-gather.8.cloned.1.call-start = ((), (), s32[]{:S(2)}) async-start(), calls=%async_computation.4 | async-start | bytes 9732096 | tf_op jit(solution)/shard_map/all_gather | solution.py:63
  9.5 126.7 %all-gather.4.cloned.1.call-start = ((), (), s32[]{:S(2)}) async-start(), calls=%async_computation.2 | async-start | bytes 9732096 | tf_op jit(solution)/shard_map/all_gather | solution.py:60
  11.4 187.3 %all-gather.6.cloned.1.call-start = ((), (), s32[]{:S(2)}) async-start(), calls=%async_computation.3 | async-start | bytes 9732096 | tf_op jit(solution)/shard_map/all_gather | solution.py:61
  13.2 425.8 %reduce-scatter.7.cloned.1.call-start = ((), (), s32[]{:S(2)}) async-start(), calls=%async_computation.5 | async-start | bytes 1769472
  97.5 103.6 %copy-start.5 = (s32[4]{0:T(128)S(1)}, s32[4]{0:T(128)}, u32[]{:S(2)}) copy-start(s32[4]{0:T(128)} %param.19) | copy-start | bytes 52
  207.6 2.8 copy-start
  210.4 270.4 %reduce-scatter.9.cloned.1.call-start = ((), (), s32[]{:S(2)}) async-start(), calls=%async_computation.6 | async-start | bytes 1769472
Sparse Core Ops, SparseCore 0:
  10.5 63.1 all-gather.7
  76.3 59.8 all-gather.3
  138.8 59.8 all-gather.5
  210.5 228.4 reduce-scatter.6
  441.4 39.2 reduce-scatter.8
where the time goes:
time: 491 us; the launch traced here: 489 us
  waiting for transfers between devices  426 us (87%)
  local copies, waits for them, and re-layouts  39.6 us (8%)
  between operations  13.8 us (3%)
  other arithmetic  6.36 us (1%)
    unnamed x7, waiting for transfers between devices  265 us
    all_gather x1, waiting for transfers between devices, shards(): lax.all_gather(up_low, 'dp', axis=1, tiled=True)  62.5 us
    all_gather x1, waiting for transfers between devices, shards(): down_all = lax.all_gather(down_low, 'dp', axis=2, tiled=True)  60.4 us
    all_gather x1, waiting for transfers between devices, shards(): lax.all_gather(gate_low, 'dp', axis=1, tiled=True)  38.7 us
    while x1, local copies, waits for them, and re-layouts, shards(): totals = lax.fori_loop(0, block_count, visit_all, totals)  23.8 us
    unnamed x11, local copies, waits for them, and re-layouts  11.1 us
  transfers between devices with their start and end apart: 5, of which 5 were waited for; matrix products, arithmetic and copies ran while one was open for 7% of the time, Pallas kernels for 0%

commit v1 on v0

v1 whole, which is shorter than its diff:
```python
import functools

import jax
import jax.numpy as jnp
from jax import lax
from jax.experimental import pallas as pl
from jax.experimental.pallas import tpu as pltpu
from jax.sharding import PartitionSpec as P

MESH = pl.DeviceIdType.MESH
NX, NY, NC, NZ = 4, 4, 2, 8
ROWS = 96
HALF = ROWS // 2
D = NX * NY * NC * ROWS
F = 768
TOK = 256
COLS = D // NZ
PIECES = 6
KINDS = 12
NSUB = 2
SUB = TOK // 2 // NSUB
STEPS = NZ - 1
NT = (((1,), (1,)), ((), ()))
NN = (((1,), (0,)), ((), ()))
GATE, UP, DOWN = (0, 2), (1, 3), (4, 5)


def dot(a, b, dims):
    return lax.dot_general(a, b, dims, preferred_element_type=jnp.float32)


def kernel(
    expert_ref,
    slot_token_ref,
    slot_gate_ref,
    tokens_ref,
    cotangent_ref,
    w_gate_ref,
    w_up_ref,
    w_down_ref,
    y_ref,
    dx_ref,
    w_all,
    d_out,
    scale_ref,
    gate_pre,
    up_pre,
    d_hidden,
    hidden,
    d_pre,
    d_up,
    part,
    send_buf,
    recv_buf,
    g_send,
    g_recv,
    r_send,
    r_recv,
):
    dp = lax.axis_index("dp")
    z = lax.axis_index("etp")
    x, y, c = dp // 8, (dp // 2) % 4, dp % 2

    def dev(xx, yy, cc, zz):
        return ((xx % NX) * 8 + (yy % NY) * 2 + cc, zz % NZ)

    right, left = dev(x, y, c, z + 1), dev(x, y, c, z + NZ - 1)
    partner = dev(x, y, 1 - c, z)

    barrier = pltpu.get_barrier_semaphore()
    greeted = (
        dev(x + 1, y, c, z),
        dev(x + 3, y, c, z),
        dev(x, y + 1, c, z),
        dev(x, y + 3, c, z),
        partner,
        right,
        left,
    )
    for peer in greeted:
        pl.semaphore_signal(barrier, inc=1, device_id=peer, device_id_type=MESH)

    own = pl.multiple_of(c * ROWS, ROWS)
    other = pl.multiple_of((1 - c) * ROWS, ROWS)
    for e in range(2):
        w_all[GATE[e], x, y, pl.ds(own, ROWS), :] = w_gate_ref[e].astype(jnp.bfloat16)
        w_all[UP[e], x, y, pl.ds(own, ROWS), :] = w_up_ref[e].astype(jnp.bfloat16)
        w_all[DOWN[e], x, y, pl.ds(own, ROWS), :] = w_down_ref[e].astype(jnp.bfloat16)

    pl.semaphore_wait(barrier, len(greeted))

    def uv(p):
        return (x, y) if p % 2 == 0 else (y, x)

    def slot(p, u, v, start, size):
        u, v = u % 4, v % 4
        a, b = (u, v) if p % 2 == 0 else (v, u)
        return w_all.at[p, a, b, pl.ds(start, size), :]

    def line(p, v, start, size):
        v = v % 4
        if p % 2 == 0:
            return w_all.at[p, :, v, pl.ds(start, size), :]
        return w_all.at[p, v, :, pl.ds(start, size), :]

    def target(p, du, dv):
        return dev(x + du, y + dv, c, z) if p % 2 == 0 else dev(x + dv, y + du, c, z)

    def sent(p, k):
        u, v = uv(p)
        low, high = own, own + HALF
        if k < 4:
            step = 1 if k % 2 == 0 else 3
            if k < 2:
                ref = slot(p, u, v, own, ROWS)
            elif k == 2:
                ref = slot(p, u + 3, v, low, HALF)
            else:
                ref = slot(p, u + 1, v, high, HALF)
            return ref, target(p, step, 0)
        if k < 8:
            step = 1 if k % 2 == 0 else 3
            if k < 6:
                ref = line(p, v, own, ROWS)
            elif k == 6:
                ref = line(p, v + 3, low, HALF)
            else:
                ref = line(p, v + 1, high, HALF)
            return ref, target(p, 0, step)
        return line(p, v + (0, 3, 1, 2)[k - 8], own, ROWS), partner

    def landed(p, k):
        u, v = uv(p)
        low, high = own, own + HALF
        if k == 0:
            return slot(p, u + 3, v, own, ROWS)
        if k == 1:
            return slot(p, u + 1, v, own, ROWS)
        if k == 2:
            return slot(p, u + 2, v, low, HALF)
        if k == 3:
            return slot(p, u + 2, v, high, HALF)
        if k == 4:
            return line(p, v + 3, own, ROWS)
        if k == 5:
            return line(p, v + 1, own, ROWS)
        if k == 6:
            return line(p, v + 2, low, HALF)
        if k == 7:
            return line(p, v + 2, high, HALF)
        return line(p, v + (0, 3, 1, 2)[k - 8], other, ROWS)

    def copy(ref, peer, p, k):
        return pltpu.make_async_remote_copy(
            src_ref=ref,
            dst_ref=ref,
            send_sem=g_send.at[p, k],
            recv_sem=g_recv.at[p, k],
            device_id=peer,
            device_id_type=MESH,
        )

    def start(pair, *kinds):
        for k in kinds:
            for p in (2 * pair, 2 * pair + 1):
                ref, peer = sent(p, k)
                copy(ref, peer, p, k).start()

    def arrive(pair, *kinds):
        for k in kinds:
            for p in (2 * pair, 2 * pair + 1):
                copy(landed(p, k), partner, p, k).wait_recv()

    def forward_dot(lhs, p, out):
        @pl.loop(0, F // 256)
        def _(n):
            cols = pl.ds(pl.multiple_of(n * 256, 256), 256)
            rhs = w_all[p, :, :, :, cols].reshape(D, 256)
            out[:, cols] = dot(lhs[...], rhs, NN)

    def make_hidden(e):
        @pl.loop(0, TOK // 32)
        def _(i):
            rows = pl.ds(pl.multiple_of(i * 32, 32), 32)
            g = gate_pre[e, rows, :]
            squash = 1.0 / (1.0 + jnp.exp(-g))
            h = g * squash * up_pre[e, rows, :] * scale_ref[e, rows, :]
            hidden[e, rows, :] = h.astype(jnp.bfloat16)

    def make_d(e):
        @pl.loop(0, TOK // 32)
        def _(i):
            rows = pl.ds(pl.multiple_of(i * 32, 32), 32)
            g = gate_pre[e, rows, :]
            dh = d_hidden[e, rows, :]
            squash = 1.0 / (1.0 + jnp.exp(-g))
            dp_ = dh * up_pre[e, rows, :] * squash * (1.0 + g * (1.0 - squash))
            d_pre[e, rows, :] = dp_.astype(jnp.bfloat16)
            d_up[e, rows, :] = (dh * (g * squash)).astype(jnp.bfloat16)

    start(0, 0, 1)
    start(1, 0, 1)

    lane = lax.broadcasted_iota(jnp.int32, (1, 512), 1)
    block = [expert_ref[i] for i in range(4)]
    of_slot = jnp.where(
        lane < 128,
        block[0],
        jnp.where(lane < 256, block[1], jnp.where(lane < 384, block[2], block[3])),
    )
    amount = slot_gate_ref[...].astype(jnp.float32) / 16.0
    for e in range(2):
        amount_e = jnp.where(of_slot == e, amount, 0.0)

        @pl.loop(0, TOK // 64)
        def _(i):
            first = pl.multiple_of(i * 64, 64)
            token = lax.broadcasted_iota(jnp.int32, (64, 512), 0) + first
            hit = jnp.where(token == slot_token_ref[...], amount_e, 0.0)
            scale_ref[e, pl.ds(first, 64), :] = jnp.sum(hit, axis=1, keepdims=True)

    arrive(0, 0, 1)
    start(0, 2, 3)

    for e in range(2):

        @pl.loop(0, TOK // 16)
        def _(i):
            rows = pl.ds(pl.multiple_of(i * 16, 16), 16)
            up_rows = cotangent_ref[rows, :].astype(jnp.float32) * scale_ref[e, rows, :]
            d_out[e, rows, :] = up_rows.astype(jnp.bfloat16)

    arrive(0, 2, 3)
    start(0, 4, 5, 8)
    arrive(1, 0, 1)
    start(1, 2, 3)
    start(2, 0, 1)
    arrive(0, 4, 5)
    start(0, 6, 7, 9, 10)
    arrive(1, 2, 3)
    start(1, 4, 5, 8)
    arrive(2, 0, 1)
    start(2, 2, 3)
    arrive(0, 6, 7)
    start(0, 11)
    arrive(0, 8, 9, 10, 11)
    forward_dot(tokens_ref, GATE[0], gate_pre.at[0])
    forward_dot(tokens_ref, UP[0], up_pre.at[0])
    make_hidden(0)
    arrive(2, 2, 3)
    arrive(1, 4, 5)
    start(2, 4, 5, 8)
    start(1, 6, 7, 9, 10)
    arrive(1, 6, 7)
    start(1, 11)
    arrive(1, 8, 9, 10, 11)
    forward_dot(tokens_ref, GATE[1], gate_pre.at[1])
    arrive(2, 4, 5)
    start(2, 6, 7, 9, 10)
    forward_dot(tokens_ref, UP[1], up_pre.at[1])
    make_hidden(1)
    arrive(2, 6, 7)
    start(2, 11)
    arrive(2, 8, 9, 10, 11)

    def weight_block(p, b):
        rows = w_all[p, b // 2, pl.ds(2 * (b % 2), 2), :, :]
        return rows.reshape(COLS, F)

    def block_y(b):
        total = dot(hidden[0], weight_block(DOWN[0], b), NT)
        part[0, b] = total + dot(hidden[1], weight_block(DOWN[1], b), NT)

    def block_dx(b):
        total = dot(d_pre[0], weight_block(GATE[0], b), NT)
        total = total + dot(d_up[0], weight_block(UP[0], b), NT)
        total = total + dot(d_pre[1], weight_block(GATE[1], b), NT)
        part[1, b] = total + dot(d_up[1], weight_block(UP[1], b), NT)

    def compute(t, s):
        count = 2 if s < 3 else 1 if s < 5 else 0
        if count == 0:
            return

        @pl.loop(0, count)
        def _(i):
            if s == 4:
                b = z
            else:
                b = lax.rem(jnp.where(i == 0, z - 1 - s + NZ, z + 1 + s), NZ)
            if t == 0:
                block_y(b)
            else:
                block_dx(b)

    def hop(t, d, h, s):
        return pltpu.make_async_remote_copy(
            src_ref=send_buf.at[t, d, h, s],
            dst_ref=recv_buf.at[t, d, h, s],
            send_sem=r_send.at[t, d, h, s],
            recv_sem=r_recv.at[t, d, h, s],
            device_id=right if d == 0 else left,
            device_id_type=MESH,
        )

    def ring(t, s):
        compute(t, s)
        for h in range(NSUB):
            for d in range(2):
                b = lax.rem(z - 1 - s + NZ, NZ) if d == 0 else lax.rem(z + 1 + s, NZ)
                first = (d * NSUB + h) * SUB
                value = part[t, b, first : first + SUB, :]
                if s > 0:
                    hop(t, d, h, s - 1).wait_recv()
                    value = value + recv_buf[t, d, h, s - 1].astype(jnp.float32)
                send_buf[t, d, h, s] = value.astype(jnp.bfloat16)
                hop(t, d, h, s).start()

    def finish(t, out):
        for h in range(NSUB):
            for d in range(2):
                first = (d * NSUB + h) * SUB
                hop(t, d, h, STEPS - 1).wait_recv()
                value = part[t, z, first : first + SUB, :]
                value = value + recv_buf[t, d, h, STEPS - 1].astype(jnp.float32)
                out[first : first + SUB, :] = value.astype(jnp.bfloat16)

    ring(0, 0)
    forward_dot(d_out.at[0], DOWN[0], d_hidden.at[0])
    ring(0, 1)
    forward_dot(d_out.at[1], DOWN[1], d_hidden.at[1])
    ring(0, 2)
    make_d(0)
    make_d(1)
    ring(1, 0)
    for s in range(3, STEPS):
        ring(0, s)
        ring(1, s - 2)
    finish(0, y_ref)
    ring(1, STEPS - 2)
    ring(1, STEPS - 1)
    finish(1, dx_ref)

    for p in range(PIECES):
        for k in range(KINDS):
            copy(sent(p, k)[0], partner, p, k).wait_send()
    for t in range(2):
        for s in range(STEPS):
            for h in range(NSUB):
                for d in range(2):
                    hop(t, d, h, s).wait_send()


def shards(tokens, cotangent, w_gate, w_up, w_down, slot_token, slot_gate, block_expert):
    vmem = pl.BlockSpec(memory_space=pltpu.VMEM)
    smem = pl.BlockSpec(memory_space=pltpu.SMEM)
    wide = (2, TOK, F)
    ring_shape = (2, 2, NSUB, STEPS)
    out = jax.ShapeDtypeStruct((TOK, COLS), jnp.bfloat16)
    return pl.pallas_call(
        kernel,
        out_shape=(out, out),
        in_specs=[smem] + [vmem] * 7,
        out_specs=(vmem, vmem),
        scratch_shapes=[
            pltpu.VMEM((PIECES, NX, NY, NC * ROWS, F), jnp.bfloat16),
            pltpu.VMEM((2, TOK, D), jnp.bfloat16),
            pltpu.VMEM((2, TOK, 1), jnp.float32),
            pltpu.VMEM(wide, jnp.float32),
            pltpu.VMEM(wide, jnp.float32),
            pltpu.VMEM(wide, jnp.float32),
            pltpu.VMEM(wide, jnp.bfloat16),
            pltpu.VMEM(wide, jnp.bfloat16),
            pltpu.VMEM(wide, jnp.bfloat16),
            pltpu.VMEM((2, NZ, TOK, COLS), jnp.float32),
            pltpu.VMEM(ring_shape + (SUB, COLS), jnp.bfloat16),
            pltpu.VMEM(ring_shape + (SUB, COLS), jnp.bfloat16),
            pltpu.SemaphoreType.DMA((PIECES, KINDS)),
            pltpu.SemaphoreType.DMA((PIECES, KINDS)),
            pltpu.SemaphoreType.DMA(ring_shape),
            pltpu.SemaphoreType.DMA(ring_shape),
        ],
        compiler_params=pltpu.CompilerParams(
            collective_id=0, has_side_effects=True, vmem_limit_bytes=63 * 1024 * 1024
        ),
    )(
        block_expert,
        slot_token.reshape(1, -1),
        slot_gate.reshape(1, -1),
        tokens,
        cotangent,
        w_gate,
        w_up,
        jnp.swapaxes(w_down, 1, 2),
    )


def solution(mesh):
    in_specs = (
        P("dp", None),
        P("dp", None),
        P(None, "dp", "etp"),
        P(None, "dp", "etp"),
        P(None, "etp", "dp"),
        P("dp"),
        P("dp"),
        P("dp"),
    )
    out_specs = (P("dp", "etp"), P("dp", "etp"))
    return jax.shard_map(shards, mesh=mesh, in_specs=in_specs, out_specs=out_specs, check_vma=False)
```

time: 491 us -> 141 us (0.29)
  waiting for transfers between devices: 426 us -> 0 us
  Pallas kernels: 0 us -> 137 us
  local copies, waits for them, and re-layouts: 39.6 us -> 3.25 us
  between operations: 13.8 us -> 0.64 us
  other arithmetic: 6.36 us -> 0 us
    unnamed x7 -> x0, waiting for transfers between devices: 265 us -> none
    all_gather x3 -> x0, waiting for transfers between devices: 162 us -> none  [the longest x1 62.5 us: shards(): lax.all_gather(up_low, 'dp', axis=1, tiled=True)]
    pallas_call x0 -> x1, Pallas kernels: none -> 137 us  [shards(): pl.pallas_call(kernel, out_shape=(out, out), in_specs=[smem] + [vmem] * 7...]
    while x1 -> x0, local copies, waits for them, and re-layouts: 23.8 us -> none  [shards(): totals = lax.fori_loop(0, block_count, visit_all, totals)]
    unnamed x11 -> x2, local copies, waits for them, and re-layouts: 11.1 us -> 3.25 us
    convert_element_type x4 -> x0, other arithmetic: 6.36 us -> none  [the longest x1 1.81 us: shards(): gate_low = w_gate.astype(jnp.bfloat16)]
  transfers between devices with their start and end apart: 5 -> 0, of which waited for: 5 -> 0; matrix products, arithmetic and copies ran while one was open for 7% -> 0% of each run, Pallas kernels for 0% -> 0%
where the time goes in v1:
time: 141 us
  Pallas kernels  137 us (97%)
  local copies, waits for them, and re-layouts  3.25 us (2%)
    pallas_call x1, Pallas kernels, shards(): pl.pallas_call(kernel, out_shape=(out, out), in_specs=[smem] + [vmem] * 7...  137 us
    unnamed x2, local copies, waits for them, and re-layouts  3.25 us

profile of v1, /device:TPU:4, one launch (start us, length us, event | category | flops | bytes accessed | tf_op | source)
XLA Modules:
  0.0 140.7 jit_solution(11155413630563665689)
XLA Ops:
  0.6 136.8 %shard_map.95 = (bf16[256,384]{1,0:T(8,128)(2,1)}, bf16[256,384]{1,0:T(8,128)(2,1)}) custom-call(s32[4]{0:T(128)} %expert_ref.1, s32[1,512]{1,0:T(1,128)} %bitcast.4, s32[1,512]{1,0:T(1,128)} %bitcast.5, bf16[256,3072]{1,0:T(8,128)(2,1)} %tokens_ref.1, bf16[256,3072]{1,0:T(8,128)(2,1)} %cotangent_ref.1, f32[2,96,768]{2,1,0:T(8,128)} %w_gate_ref.1, ...), custom_call_target="tpu_custom_call" | custom-call | tf_op jit(solution)/shard_map/pallas_call | solution.py:360
  137.4 1.6 %copy.12 = bf16[256,384]{1,0:T(8,128)(2,1)} copy(bf16[256,384]{1,0:T(8,128)(2,1)} %get-tuple-element.4) | data formatting | bytes 393216
  139.1 1.6 %copy.13 = bf16[256,384]{1,0:T(8,128)(2,1)} copy(bf16[256,384]{1,0:T(8,128)(2,1)} %get-tuple-element.5) | data formatting | bytes 393216

commit v2 on v1

--- a/solution.py
+++ b/solution.py
@@ -15,8 +15,8 @@
 F = 768
 TOK = 256
 COLS = D // NZ
-PIECES = 6
-KINDS = 12
+PAIRS = (((0, 1), 0, ROWS), ((2, 3), 0, ROWS), ((4, 5), 0, ROWS))
+KINDS = 19
 NSUB = 2
 SUB = TOK // 2 // NSUB
 STEPS = NZ - 1
@@ -33,13 +33,15 @@
     expert_ref,
     slot_token_ref,
     slot_gate_ref,
+    tokens_hbm,
+    cotangent_hbm,
+    w_gate_hbm,
+    w_up_hbm,
+    w_down_hbm,
+    out_ref,
     tokens_ref,
     cotangent_ref,
-    w_gate_ref,
-    w_up_ref,
-    w_down_ref,
-    y_ref,
-    dx_ref,
+    masters,
     w_all,
     d_out,
     scale_ref,
@@ -56,6 +58,7 @@
     g_recv,
     r_send,
     r_recv,
+    l_sem,
 ):
     dp = lax.axis_index("dp")
     z = lax.axis_index("etp")
@@ -80,102 +83,86 @@
     for peer in greeted:
         pl.semaphore_signal(barrier, inc=1, device_id=peer, device_id_type=MESH)
 
-    own = pl.multiple_of(c * ROWS, ROWS)
-    other = pl.multiple_of((1 - c) * ROWS, ROWS)
-    for e in range(2):
-        w_all[GATE[e], x, y, pl.ds(own, ROWS), :] = w_gate_ref[e].astype(jnp.bfloat16)
-        w_all[UP[e], x, y, pl.ds(own, ROWS), :] = w_up_ref[e].astype(jnp.bfloat16)
-        w_all[DOWN[e], x, y, pl.ds(own, ROWS), :] = w_down_ref[e].astype(jnp.bfloat16)
-
-    pl.semaphore_wait(barrier, len(greeted))
-
-    def uv(p):
-        return (x, y) if p % 2 == 0 else (y, x)
-
-    def slot(p, u, v, start, size):
-        u, v = u % 4, v % 4
-        a, b = (u, v) if p % 2 == 0 else (v, u)
-        return w_all.at[p, a, b, pl.ds(start, size), :]
-
-    def line(p, v, start, size):
-        v = v % 4
-        if p % 2 == 0:
-            return w_all.at[p, :, v, pl.ds(start, size), :]
-        return w_all.at[p, v, :, pl.ds(start, size), :]
-
-    def target(p, du, dv):
-        return dev(x + du, y + dv, c, z) if p % 2 == 0 else dev(x + dv, y + du, c, z)
-
-    def sent(p, k):
-        u, v = uv(p)
-        low, high = own, own + HALF
+    loads = [
+        pltpu.make_async_copy(w_gate_hbm, masters.at[0], l_sem.at[0]),
+        pltpu.make_async_copy(w_up_hbm, masters.at[1], l_sem.at[1]),
+        pltpu.make_async_copy(w_down_hbm, masters.at[2], l_sem.at[2]),
+        pltpu.make_async_copy(cotangent_hbm, cotangent_ref, l_sem.at[3]),
+        pltpu.make_async_copy(tokens_hbm, tokens_ref, l_sem.at[4]),
+    ]
+    for load in loads:
+        load.start()
+
+    def cast(m, name, e):
+        w_all[name[e], x, y, c, :, :] = masters[m, e].astype(jnp.bfloat16)
+
+    def barrier_wait():
+        pl.semaphore_wait(barrier, len(greeted))
+
+    def place(pair, i, u, v, cc, first, size):
+        m, r0, _ = PAIRS[pair]
+        rows = pl.ds(r0 + first, size)
+        if i == 0:
+            return w_all.at[m[i], u, v, cc, rows, :]
+        return w_all.at[m[i], v, u, cc, rows, :]
+
+    def leg(pair, i, k):
+        size = PAIRS[pair][2]
+        half = size // 2
+        u, v = (x, y) if i == 0 else (y, x)
+        up = 1 if k % 2 == 0 else 3
+        down = 4 - up
+
+        def at(du, dv, first=0, count=size, cc=c):
+            return place(pair, i, (u + du) % 4, (v + dv) % 4, cc, first, count)
+
+        def line(part, dv, first=0, count=size, cc=c):
+            uu = pl.ds(0, 4) if part is None else pl.ds(2 * part, 2)
+            return place(pair, i, uu, (v + dv) % 4, cc, first, count)
+
+        def peer(du, dv):
+            return dev(x + du, y + dv, c, z) if i == 0 else dev(x + dv, y + du, c, z)
+
+        if k < 2:
+            return at(0, 0), peer(up, 0), at(down, 0)
         if k < 4:
-            step = 1 if k % 2 == 0 else 3
-            if k < 2:
-                ref = slot(p, u, v, own, ROWS)
-            elif k == 2:
-                ref = slot(p, u + 3, v, low, HALF)
-            else:
-                ref = slot(p, u + 1, v, high, HALF)
-            return ref, target(p, step, 0)
+            first = half * (k % 2)
+            return at(down, 0, first, half), peer(up, 0), at(2, 0, first, half)
         if k < 8:
-            step = 1 if k % 2 == 0 else 3
-            if k < 6:
-                ref = line(p, v, own, ROWS)
-            elif k == 6:
-                ref = line(p, v + 3, low, HALF)
-            else:
-                ref = line(p, v + 1, high, HALF)
-            return ref, target(p, 0, step)
-        return line(p, v + (0, 3, 1, 2)[k - 8], own, ROWS), partner
-
-    def landed(p, k):
-        u, v = uv(p)
-        low, high = own, own + HALF
-        if k == 0:
-            return slot(p, u + 3, v, own, ROWS)
-        if k == 1:
-            return slot(p, u + 1, v, own, ROWS)
-        if k == 2:
-            return slot(p, u + 2, v, low, HALF)
-        if k == 3:
-            return slot(p, u + 2, v, high, HALF)
-        if k == 4:
-            return line(p, v + 3, own, ROWS)
-        if k == 5:
-            return line(p, v + 1, own, ROWS)
-        if k == 6:
-            return line(p, v + 2, low, HALF)
-        if k == 7:
-            return line(p, v + 2, high, HALF)
-        return line(p, v + (0, 3, 1, 2)[k - 8], other, ROWS)
-
-    def copy(ref, peer, p, k):
+            part = (k - 4) // 2
+            return line(part, 0), peer(0, up), line(part, down)
+        if k < 12:
+            part, first = (k - 8) // 2, half * (k % 2)
+            return line(part, down, first, half), peer(0, up), line(part, 2, first, half)
+        part, dv = ((None, 0), (0, 3), (0, 1), (1, 3), (1, 1), (0, 2), (1, 2))[k - 12]
+        return line(part, dv), partner, line(part, dv, cc=1 - c)
+
+    def copy(ref, peer, pair, i, k):
         return pltpu.make_async_remote_copy(
             src_ref=ref,
             dst_ref=ref,
-            send_sem=g_send.at[p, k],
-            recv_sem=g_recv.at[p, k],
+            send_sem=g_send.at[2 * pair + i, k],
+            recv_sem=g_recv.at[2 * pair + i, k],
             device_id=peer,
             device_id_type=MESH,
         )
 
     def start(pair, *kinds):
         for k in kinds:
-            for p in (2 * pair, 2 * pair + 1):
-                ref, peer = sent(p, k)
-                copy(ref, peer, p, k).start()
+            for i in range(2):
+                ref, peer, _ = leg(pair, i, k)
+                copy(ref, peer, pair, i, k).start()
 
     def arrive(pair, *kinds):
         for k in kinds:
-            for p in (2 * pair, 2 * pair + 1):
-                copy(landed(p, k), partner, p, k).wait_recv()
+            for i in range(2):
+                copy(leg(pair, i, k)[2], partner, pair, i, k).wait_recv()
 
     def forward_dot(lhs, p, out):
         @pl.loop(0, F // 256)
         def _(n):
             cols = pl.ds(pl.multiple_of(n * 256, 256), 256)
-            rhs = w_all[p, :, :, :, cols].reshape(D, 256)
+            rhs = w_all[p, :, :, :, :, cols].reshape(D, 256)
             out[:, cols] = dot(lhs[...], rhs, NN)
 
     def make_hidden(e):
@@ -198,8 +185,19 @@
             d_pre[e, rows, :] = dp_.astype(jnp.bfloat16)
             d_up[e, rows, :] = (dh * (g * squash)).astype(jnp.bfloat16)
 
+    loads[0].wait()
+    cast(0, GATE, 0)
+    loads[1].wait()
+    cast(1, UP, 0)
+    barrier_wait()
     start(0, 0, 1)
+    cast(0, GATE, 1)
+    cast(1, UP, 1)
     start(1, 0, 1)
+    loads[2].wait()
+    cast(2, DOWN, 0)
+    cast(2, DOWN, 1)
+    start(2, 0, 1)
 
     lane = lax.broadcasted_iota(jnp.int32, (1, 512), 1)
     block = [expert_ref[i] for i in range(4)]
@@ -221,7 +219,14 @@
 
     arrive(0, 0, 1)
     start(0, 2, 3)
-
+    arrive(1, 0, 1)
+    start(1, 2, 3)
+    arrive(0, 2, 3)
+    start(0, 4, 5, 6, 7, 12)
+    arrive(2, 0, 1)
+    start(2, 2, 3)
+    arrive(1, 2, 3)
+    loads[3].wait()
     for e in range(2):
 
         @pl.loop(0, TOK // 16)
@@ -230,41 +235,46 @@
             up_rows = cotangent_ref[rows, :].astype(jnp.float32) * scale_ref[e, rows, :]
             d_out[e, rows, :] = up_rows.astype(jnp.bfloat16)
 
-    arrive(0, 2, 3)
-    start(0, 4, 5, 8)
-    arrive(1, 0, 1)
-    start(1, 2, 3)
-    start(2, 0, 1)
+    loads[4].wait()
     arrive(0, 4, 5)
-    start(0, 6, 7, 9, 10)
-    arrive(1, 2, 3)
-    start(1, 4, 5, 8)
-    arrive(2, 0, 1)
-    start(2, 2, 3)
+    start(0, 8, 9, 13, 14)
     arrive(0, 6, 7)
-    start(0, 11)
-    arrive(0, 8, 9, 10, 11)
+    start(0, 10, 11, 15, 16)
+    start(1, 4, 5, 6, 7, 12)
+    arrive(2, 2, 3)
+    arrive(0, 8, 9)
+    start(0, 17)
+    arrive(0, 10, 11)
+    start(0, 18)
+    arrive(0, 12, 13, 14, 15, 16, 17, 18)
     forward_dot(tokens_ref, GATE[0], gate_pre.at[0])
     forward_dot(tokens_ref, UP[0], up_pre.at[0])
     make_hidden(0)
-    arrive(2, 2, 3)
     arrive(1, 4, 5)
-    start(2, 4, 5, 8)
-    start(1, 6, 7, 9, 10)
+    start(1, 8, 9, 13, 14)
     arrive(1, 6, 7)
-    start(1, 11)
-    arrive(1, 8, 9, 10, 11)
+    start(1, 10, 11, 15, 16)
+    start(2, 4, 5, 6, 7, 12)
+    arrive(1, 8, 9)
+    start(1, 17)
+    arrive(1, 10, 11)
+    start(1, 18)
+    arrive(1, 12, 13, 14, 15, 16, 17, 18)
     forward_dot(tokens_ref, GATE[1], gate_pre.at[1])
-    arrive(2, 4, 5)
-    start(2, 6, 7, 9, 10)
     forward_dot(tokens_ref, UP[1], up_pre.at[1])
     make_hidden(1)
+    arrive(2, 4, 5)
+    start(2, 8, 9, 13, 14)
     arrive(2, 6, 7)
-    start(2, 11)
-    arrive(2, 8, 9, 10, 11)
+    start(2, 10, 11, 15, 16)
+    arrive(2, 8, 9)
+    start(2, 17)
+    arrive(2, 10, 11)
+    start(2, 18)
+    arrive(2, 12, 13, 14, 15, 16, 17, 18)
 
     def weight_block(p, b):
-        rows = w_all[p, b // 2, pl.ds(2 * (b % 2), 2), :, :]
+        rows = w_all[p, b // 2, pl.ds(2 * (b % 2), 2), :, :, :]
         return rows.reshape(COLS, F)
 
     def block_y(b):
@@ -316,14 +326,14 @@
                 send_buf[t, d, h, s] = value.astype(jnp.bfloat16)
                 hop(t, d, h, s).start()
 
-    def finish(t, out):
+    def finish(t):
         for h in range(NSUB):
             for d in range(2):
                 first = (d * NSUB + h) * SUB
                 hop(t, d, h, STEPS - 1).wait_recv()
                 value = part[t, z, first : first + SUB, :]
                 value = value + recv_buf[t, d, h, STEPS - 1].astype(jnp.float32)
-                out[first : first + SUB, :] = value.astype(jnp.bfloat16)
+                out_ref[t, first : first + SUB, :] = value.astype(jnp.bfloat16)
 
     ring(0, 0)
     forward_dot(d_out.at[0], DOWN[0], d_hidden.at[0])
@@ -336,14 +346,15 @@
     for s in range(3, STEPS):
         ring(0, s)
         ring(1, s - 2)
-    finish(0, y_ref)
+    finish(0)
     ring(1, STEPS - 2)
     ring(1, STEPS - 1)
-    finish(1, dx_ref)
-
-    for p in range(PIECES):
-        for k in range(KINDS):
-            copy(sent(p, k)[0], partner, p, k).wait_send()
+    finish(1)
+
+    for pair in range(len(PAIRS)):
+        for i in range(2):
+            for k in range(KINDS):
+                copy(leg(pair, i, k)[0], partner, pair, i, k).wait_send()
     for t in range(2):
         for s in range(STEPS):
             for h in range(NSUB):
@@ -356,14 +367,18 @@
     smem = pl.BlockSpec(memory_space=pltpu.SMEM)
     wide = (2, TOK, F)
     ring_shape = (2, 2, NSUB, STEPS)
-    out = jax.ShapeDtypeStruct((TOK, COLS), jnp.bfloat16)
-    return pl.pallas_call(
+    hbm = pl.BlockSpec(memory_space=pl.ANY)
+    sems = (2 * len(PAIRS), KINDS)
+    out = pl.pallas_call(
         kernel,
-        out_shape=(out, out),
-        in_specs=[smem] + [vmem] * 7,
-        out_specs=(vmem, vmem),
+        out_shape=jax.ShapeDtypeStruct((2, TOK, COLS), jnp.bfloat16),
+        in_specs=[smem] + [vmem] * 2 + [hbm] * 5,
+        out_specs=vmem,
         scratch_shapes=[
-            pltpu.VMEM((PIECES, NX, NY, NC * ROWS, F), jnp.bfloat16),
+            pltpu.VMEM((TOK, D), jnp.bfloat16),
+            pltpu.VMEM((TOK, D), jnp.bfloat16),
+            pltpu.VMEM((3, 2, ROWS, F), jnp.float32),
+            pltpu.VMEM((6, NX, NY, NC, ROWS, F), jnp.bfloat16),
             pltpu.VMEM((2, TOK, D), jnp.bfloat16),
             pltpu.VMEM((2, TOK, 1), jnp.float32),
             pltpu.VMEM(wide, jnp.float32),
@@ -375,10 +390,11 @@
             pltpu.VMEM((2, NZ, TOK, COLS), jnp.float32),
             pltpu.VMEM(ring_shape + (SUB, COLS), jnp.bfloat16),
             pltpu.VMEM(ring_shape + (SUB, COLS), jnp.bfloat16),
-            pltpu.SemaphoreType.DMA((PIECES, KINDS)),
-            pltpu.SemaphoreType.DMA((PIECES, KINDS)),
+            pltpu.SemaphoreType.DMA(sems),
+            pltpu.SemaphoreType.DMA(sems),
             pltpu.SemaphoreType.DMA(ring_shape),
             pltpu.SemaphoreType.DMA(ring_shape),
+            pltpu.SemaphoreType.DMA((5,)),
         ],
         compiler_params=pltpu.CompilerParams(
             collective_id=0, has_side_effects=True, vmem_limit_bytes=63 * 1024 * 1024
@@ -393,6 +409,7 @@
         w_up,
         jnp.swapaxes(w_down, 1, 2),
     )
+    return out[0], out[1]
 
 
 def solution(mesh):

time: 141 us -> 130 us (0.922)
  Pallas kernels: 137 us -> 127 us
  local copies, waits for them, and re-layouts: 3.25 us -> 1.8 us
    pallas_call x1, Pallas kernels: 137 us -> 127 us  [shards(): pl.pallas_call(kernel, out_shape=jax.ShapeDtypeStruct((2, TOK, COLS), jnp...]
    unnamed x2 -> x0, local copies, waits for them, and re-layouts: 3.25 us -> none
    squeeze x0 -> x1, local copies, waits for them, and re-layouts: none -> 1.8 us  [shards(): return (out[0], out[1])]
where the time goes in v2:
time: 130 us
  Pallas kernels  127 us (98%)
  local copies, waits for them, and re-layouts  1.8 us (1%)
    pallas_call x1, Pallas kernels, shards(): pl.pallas_call(kernel, out_shape=jax.ShapeDtypeStruct((2, TOK, COLS), jnp...  127 us

profile of v2, /device:TPU:4, one launch (start us, length us, event | category | flops | bytes accessed | tf_op | source)
XLA Modules:
  0.0 129.7 jit_solution(11433047690327955750)
XLA Ops:
  0.6 127.3 %shard_map.95 = bf16[2,256,384]{2,1,0:T(8,128)(2,1)} custom-call(s32[4]{0:T(128)} %expert_ref.1, s32[1,512]{1,0:T(1,128)} %bitcast.8, s32[1,512]{1,0:T(1,128)} %bitcast.9, bf16[256,3072]{1,0:T(8,128)(2,1)} %tokens_hbm.1, bf16[256,3072]{1,0:T(8,128)(2,1)} %cotangent_hbm.1, f32[2,96,768]{2,1,0:T(8,128)} %w_gate_hbm.1, f32[2,96,768]{2,1,0:T(8,128)} %w_up_hbm.1, ...), custom_call_target="tpu_custom_call" | custom-call | tf_op jit(solution)/shard_map/pallas_call | solution.py:372
  127.9 1.8 %slice_bitcast_fusion = (bf16[256,384]{1,0:T(8,128)(2,1)}, bf16[256,384]{1,0:T(8,128)(2,1)}) fusion(bf16[2,256,384]{2,1,0:T(8,128)(2,1)} %shard_map.95), kind=kLoop, calls=%fused_computation | loop fusion | bytes 786432 | tf_op jit(solution)/shard_map/squeeze | solution.py:412

commit v3 on v0

v3 whole, which is shorter than its diff:
```python
import functools

import jax
import jax.numpy as jnp
from jax import lax
from jax.experimental import pallas as pl
from jax.experimental.pallas import tpu as pltpu
from jax.sharding import PartitionSpec as P

MESH = pl.DeviceIdType.MESH
NX, NY, NC, NZ = 4, 4, 2, 8
ROWS = 96
HALF = ROWS // 2
D = NX * NY * NC * ROWS
F = 768
TOK = 256
COLS = D // NZ
GROUPS = 3
GROUP = ROWS // GROUPS
GCOLS = COLS // GROUPS
GK = D // GROUPS
ALL, LOW, HIGH, OWN, NEAR, FAR = range(6)


def kinds_of(parts):
    kinds = [(name, ALL, sign) for name in ("near", "near2") for sign in (1, 3)]
    kinds += [(name, part, sign) for name in ("turn", "turn2") for part in parts for sign in (1, 3)]
    return kinds + [("core", ALL, step) for step in (0, 3, 1, 2)]


PAIRS = (
    ((0, 1), 0, ROWS, kinds_of((OWN, NEAR, FAR))),
    ((2, 3), 0, ROWS, kinds_of((LOW, HIGH))),
    ((4, 5), 0, GROUP, kinds_of((ALL,))),
    ((4, 5), GROUP, GROUP, kinds_of((ALL,))),
    ((4, 5), 2 * GROUP, GROUP, kinds_of((ALL,))),
)
FIRST = [2 * sum(len(pair[3]) for pair in PAIRS[:n]) for n in range(len(PAIRS) + 1)]
COPIES = FIRST[-1]
HOPS = NZ // 2
X_PARTS = 4
Y_PARTS = 2
NT = (((1,), (1,)), ((), ()))
NN = (((1,), (0,)), ((), ()))
GATE, UP, DOWN = (0, 2), (1, 3), (4, 5)


def dot(a, b, dims):
    return lax.dot_general(a, b, dims, preferred_element_type=jnp.float32)


def kernel(
    expert_ref,
    slot_token_hbm,
    slot_gate_hbm,
    tokens_hbm,
    cotangent_hbm,
    w_gate_hbm,
    w_up_hbm,
    w_down_hbm,
    out_ref,
    slot_token_ref,
    slot_gate_ref,
    tokens_ref,
    cotangent_ref,
    masters,
    w_all,
    perm,
    turned,
    d_out,
    scale_ref,
    pre,
    d_hidden,
    hidden,
    d_pre,
    d_up,
    part_y,
    part_x,
    y_rows,
    y_send,
    y_recv,
    x_send,
    x_recv,
    g_send,
    g_recv,
    ys_sem,
    yr_sem,
    xs_sem,
    xr_sem,
    l_sem,
):
    dp = lax.axis_index("dp")
    z = lax.axis_index("etp")
    x, y, c = dp // 8, (dp // 2) % 4, dp % 2

    def dev(xx, yy, cc, zz):
        return ((xx % NX) * 8 + (yy % NY) * 2 + cc, zz % NZ)

    right, left = dev(x, y, c, z + 1), dev(x, y, c, z + NZ - 1)
    partner = dev(x, y, 1 - c, z)

    barrier = pltpu.get_barrier_semaphore()
    greeted = (
        dev(x + 1, y, c, z),
        dev(x + 3, y, c, z),
        dev(x, y + 1, c, z),
        dev(x, y + 3, c, z),
        partner,
        right,
        left,
    )
    for peer in greeted:
        pl.semaphore_signal(barrier, inc=1, device_id=peer, device_id_type=MESH)

    loads = []
    for src, dst in (
        (w_gate_hbm.at[0], masters.at[0, 0]),
        (w_up_hbm.at[0], masters.at[1, 0]),
        (w_gate_hbm.at[1], masters.at[0, 1]),
        (w_up_hbm.at[1], masters.at[1, 1]),
        (w_down_hbm, masters.at[2]),
        (slot_token_hbm, slot_token_ref),
        (slot_gate_hbm, slot_gate_ref),
        (cotangent_hbm, cotangent_ref),
        (tokens_hbm, tokens_ref),
    ):
        loads.append(pltpu.make_async_copy(src, dst, l_sem.at[len(loads)]))
        loads[-1].start()

    def cast(m, name, e):
        w_all[name[e], x // 2, x % 2, y // 2, y % 2, c, :, :] = masters[m, e].astype(jnp.bfloat16)

    def barrier_wait():
        pl.semaphore_wait(barrier, len(greeted))

    whole = slice(None)

    def slot(u):
        return (u % 4) // 2, u % 2

    def leg(pair, i, kind):
        name, part, step = kind
        m, r0, size, _ = PAIRS[pair]
        half = size // 2
        u, v = (x, y) if i == 0 else (y, x)
        back = 4 - step
        first = half if step == 3 else 0
        us = {
            ALL: (whole, whole),
            LOW: (0, whole),
            HIGH: (1, whole),
            OWN: slot(u),
            NEAR: (whole, (u + 1) % 2),
            FAR: slot(u + 2),
        }[part]

        def at(uu, vv, start=0, count=size, cc=c):
            where = uu + vv if i == 0 else vv + uu
            return w_all.at[(m[i],) + where + (cc, pl.ds(r0 + start, count), whole)]

        def peer(du, dv):
            return dev(x + du, y + dv, c, z) if i == 0 else dev(x + dv, y + du, c, z)

        if name == "near":
            return at(slot(u), slot(v)), peer(step, 0), at(slot(u + back), slot(v))
        if name == "near2":
            mine = at(slot(u + back), slot(v), first, half)
            return mine, peer(step, 0), at(slot(u + 2), slot(v), first, half)
        if name == "turn":
            return at(us, slot(v)), peer(0, step), at(us, slot(v + back))
        if name == "turn2":
            mine = at(us, slot(v + back), first, half)
            return mine, peer(0, step), at(us, slot(v + 2), first, half)
        return at(us, slot(v + step)), partner, at(us, slot(v + step), cc=1 - c)

    def copy(ref, peer, pair, i, kind):
        kinds = PAIRS[pair][3]
        at = FIRST[pair] + i * len(kinds) + kinds.index(kind)
        return pltpu.make_async_remote_copy(
            src_ref=ref,
            dst_ref=ref,
            send_sem=g_send.at[at],
            recv_sem=g_recv.at[at],
            device_id=peer,
            device_id_type=MESH,
        )

    def start(pair, name, part=ALL, steps=(1, 3)):
        for step in steps:
            for i in range(2):
                ref, peer, _ = leg(pair, i, (name, part, step))
                copy(ref, peer, pair, i, (name, part, step)).start()

    def arrive(pair, name, part=ALL, steps=(1, 3)):
        for step in steps:
            for i in range(2):
                copy(leg(pair, i, (name, part, step))[2], partner, pair, i, (name, part, step)).wait_recv()

    def forward(first):
        @pl.loop(0, 2 * (F // 256))
        def _(j):
            m = first + j // (F // 256)
            cols = pl.ds(pl.multiple_of((j % (F // 256)) * 256, 256), 256)
            rhs = w_all[m, :, :, :, :, :, :, cols].reshape(D, 256)
            pre[m, :, cols] = dot(tokens_ref[...], rhs, NN)

    def add_d_hidden(g):
        @pl.loop(0, 2 * (F // 256))
        def _(j):
            e = j // (F // 256)
            cols = pl.ds(pl.multiple_of((j % (F // 256)) * 256, 256), 256)
            rhs = w_all[4 + e, :, :, :, :, :, pl.ds(g * GROUP, GROUP), cols].reshape(GK, 256)
            total = dot(d_out[e, g], rhs, NN)
            if g > 0:
                total = total + d_hidden[e, :, cols]
            d_hidden[e, :, cols] = total

    def make_hidden(e):
        @pl.loop(0, TOK // 32)
        def _(i):
            rows = pl.ds(pl.multiple_of(i * 32, 32), 32)
            gate = pre[2 * e, rows, :]
            squash = 1.0 / (1.0 + jnp.exp(-gate))
            h = gate * squash * pre[2 * e + 1, rows, :] * scale_ref[e, rows, :]
            hidden[e, rows, :] = h.astype(jnp.bfloat16)

    def make_d():
        @pl.loop(0, 2 * (TOK // 32))
        def _(j):
            e = j // (TOK // 32)
            rows = pl.ds(pl.multiple_of((j % (TOK // 32)) * 32, 32), 32)
            gate = pre[2 * e, rows, :]
            dh = d_hidden[e, rows, :]
            squash = 1.0 / (1.0 + jnp.exp(-gate))
            before = dh * pre[2 * e + 1, rows, :] * squash * (1.0 + gate * (1.0 - squash))
            d_pre[e, rows, :] = before.astype(jnp.bfloat16)
            d_up[e, rows, :] = (dh * (gate * squash)).astype(jnp.bfloat16)

    loads[0].wait()
    cast(0, GATE, 0)
    loads[1].wait()
    cast(1, UP, 0)
    barrier_wait()
    start(0, "near")
    start(0, "turn", OWN)
    loads[2].wait()
    cast(0, GATE, 1)
    loads[3].wait()
    cast(1, UP, 1)
    start(1, "near")
    loads[4].wait()
    cast(2, DOWN, 0)
    cast(2, DOWN, 1)

    loads[5].wait()
    loads[6].wait()
    lane = lax.broadcasted_iota(jnp.int32, (1, 512), 1)
    block = [expert_ref[i] for i in range(4)]
    of_slot = jnp.where(
        lane < 128,
        block[0],
        jnp.where(lane < 256, block[1], jnp.where(lane < 384, block[2], block[3])),
    )
    amount = slot_gate_ref[...].astype(jnp.float32) / 16.0
    for e in range(2):
        amount_e = jnp.where(of_slot == e, amount, 0.0)

        @pl.loop(0, TOK // 64)
        def _(i):
            first = pl.multiple_of(i * 64, 64)
            token = lax.broadcasted_iota(jnp.int32, (64, 512), 0) + first
            hit = jnp.where(token == slot_token_ref[...], amount_e, 0.0)
            scale_ref[e, pl.ds(first, 64), :] = jnp.sum(hit, axis=1, keepdims=True)

    row = lax.broadcasted_iota(jnp.int32, (COLS, COLS), 0)
    col = lax.broadcasted_iota(jnp.int32, (COLS, COLS), 1)
    source = ((col >> 5) & 3) * ROWS + (col >> 7) * GROUP + (col & 31)
    perm[...] = jnp.where(row == source, 1.0, 0.0).astype(jnp.bfloat16)

    arrive(0, "near")
    start(0, "near2")
    start(0, "turn", NEAR)
    arrive(0, "turn", OWN)
    start(0, "turn2", OWN)
    arrive(1, "near")
    start(1, "near2")
    for g in range(GROUPS):
        start(2 + g, "near")
    arrive(0, "near2")
    start(0, "turn", FAR)
    start(0, "core", steps=(0,))
    loads[7].wait()

    @pl.loop(0, NZ)
    def _(b):
        block = cotangent_ref[:, pl.ds(pl.multiple_of(b * COLS, COLS), COLS)]
        block = dot(block, perm[...], NN).astype(jnp.bfloat16)
        cols = pl.ds(pl.multiple_of(b * GCOLS, GCOLS), GCOLS)
        for g in range(GROUPS):
            turned[g, :, cols] = block[:, g * GCOLS : (g + 1) * GCOLS]

    for e in range(2):
        for g in range(GROUPS):

            @pl.loop(0, TOK // 32)
            def _(i):
                rows = pl.ds(pl.multiple_of(i * 32, 32), 32)
                value = turned[g, rows, :].astype(jnp.float32) * scale_ref[e, rows, :]
                d_out[e, g, rows, :] = value.astype(jnp.bfloat16)

    loads[8].wait()

    def all_y(g):
        @pl.loop(0, NX)
        def _(n):
            total = 0.0
            for e in range(2):
                rows = w_all[4 + e, n // 2, n % 2, :, :, :, pl.ds(g * GROUP, GROUP), :]
                total = total + dot(hidden[e], rows.reshape(2 * GCOLS, F), NT)
            part_y[g, 2 * n] = total[:, :GCOLS]
            part_y[g, 2 * n + 1] = total[:, GCOLS:]

    def hop(buffers, at):
        src, dst, send_sem, recv_sem = buffers
        return pltpu.make_async_remote_copy(
            src_ref=src.at[at],
            dst_ref=dst.at[at],
            send_sem=send_sem.at[at],
            recv_sem=recv_sem.at[at],
            device_id=right if at[-3] == 0 else left,
            device_id_type=MESH,
        )

    def far_first(d, h, parts):
        return (h < parts // 2) == (d == 0)

    def pieces_at(parts, step):
        order = []
        for n in range(parts):
            for d in range(2):
                h = (n + parts // 2) % parts if d == 0 else n
                if step > 0 or far_first(d, h, parts):
                    order.append((d, h))
        if step == 0:
            order = [(d, h) for h in range(parts) for d in range(2) if far_first(d, h, parts)]
        return order

    def ring(buffers, own, lead, parts, step):
        size = TOK // parts
        for d, h in pieces_at(parts, step):
            gap = HOPS - step
            b = lax.rem(z + gap, NZ) if d == 0 else lax.rem(z + NZ - gap, NZ)
            value = own[b, h * size : (h + 1) * size, :]
            if step > 1 or (step == 1 and far_first(d, h, parts)):
                before = lead + (d, h, step - 1)
                hop(buffers, before).wait_recv()
                value = value + buffers[1][before].astype(jnp.float32)
            at = lead + (d, h, step)
            buffers[0][at] = value.astype(jnp.bfloat16)
            hop(buffers, at).start()

    def collect(buffers, own, lead, parts, h):
        size = TOK // parts
        value = own[z, h * size : (h + 1) * size, :]
        for d in range(2):
            at = lead + (d, h, HOPS - 1)
            hop(buffers, at).wait_recv()
            value = value + buffers[1][at].astype(jnp.float32)
        return value.astype(jnp.bfloat16)

    def release(buffers, lead, parts):
        for step in range(HOPS):
            for d, h in pieces_at(parts, step):
                hop(buffers, lead + (d, h, step)).wait_send()

    y_buffers = (y_send, y_recv, ys_sem, yr_sem)
    x_buffers = (x_send, x_recv, xs_sem, xr_sem)

    def ring_y(g, step):
        ring(y_buffers, part_y.at[g], (g,), Y_PARTS, step)

    def end_y(g):
        size = TOK // Y_PARTS
        for h in range(Y_PARTS):
            rows = collect(y_buffers, part_y.at[g], (g,), Y_PARTS, h)
            y_rows[h * size : (h + 1) * size, g * GCOLS : (g + 1) * GCOLS] = rows

    def ring_x(step):
        ring(x_buffers, part_x, (), X_PARTS, step)

    def end_x():
        size = TOK // X_PARTS
        for n in range(X_PARTS):
            h = n // 2 + (n % 2) * (X_PARTS // 2)
            rows = collect(x_buffers, part_x, (), X_PARTS, h)
            out_ref[1, h * size : (h + 1) * size, :] = rows

    def weight_block(p, b):
        rows = w_all[p, b // 4, (b // 2) % 2, b % 2, :, :, :, :]
        return rows.reshape(COLS, F)

    def compute_dx(gap):
        @pl.loop(0, 1 if gap in (0, HOPS) else 2)
        def _(i):
            b = lax.rem(jnp.where(i == 0, z + gap, z + NZ - gap), NZ)
            total = dot(d_pre[0], weight_block(GATE[0], b), NT)
            total = total + dot(d_up[0], weight_block(UP[0], b), NT)
            total = total + dot(d_pre[1], weight_block(GATE[1], b), NT)
            part_x[b] = total + dot(d_up[1], weight_block(UP[1], b), NT)

    arrive(0, "turn", NEAR)
    start(0, "turn2", NEAR)
    for g in range(GROUPS):
        arrive(2 + g, "near")
        start(2 + g, "near2")
    arrive(1, "near2")
    arrive(0, "turn", FAR)
    start(0, "turn2", FAR)
    start(1, "turn", LOW)
    start(1, "turn", HIGH)
    start(1, "core", steps=(0,))
    start(0, "core", steps=(3, 1))
    for part in (OWN, NEAR, FAR):
        arrive(0, "turn2", part)
    start(0, "core", steps=(2,))
    for g in range(GROUPS):
        arrive(2 + g, "near2")
    arrive(0, "core", steps=(0, 3, 1, 2))
    forward(0)
    make_hidden(0)
    arrive(1, "turn", LOW)
    start(1, "turn2", LOW)
    arrive(1, "turn", HIGH)
    start(1, "turn2", HIGH)
    start(1, "core", steps=(3, 1))
    start(2, "turn")
    start(3, "turn")
    for g in range(GROUPS):
        start(2 + g, "core", steps=(0,))
    arrive(1, "turn2", LOW)
    arrive(1, "turn2", HIGH)
    start(1, "core", steps=(2,))
    arrive(2, "turn")
    start(2, "turn2")
    start(4, "turn")
    start(2, "core", steps=(3, 1))
    arrive(1, "core", steps=(0, 3, 1, 2))
    forward(2)
    make_hidden(1)
    arrive(3, "turn")
    start(3, "turn2")
    start(3, "core", steps=(3, 1))
    arrive(2, "turn2")
    start(2, "core", steps=(2,))
    arrive(2, "core", steps=(0, 3, 1, 2))
    all_y(0)
    ring_y(0, 0)
    arrive(4, "turn")
    start(4, "turn2")
    start(4, "core", steps=(3, 1))
    add_d_hidden(0)
    ring_y(0, 1)
    arrive(3, "turn2")
    start(3, "core", steps=(2,))
    arrive(3, "core", steps=(0, 3, 1, 2))
    all_y(1)
    ring_y(1, 0)
    arrive(4, "turn2")
    start(4, "core", steps=(2,))
    ring_y(0, 2)
    add_d_hidden(1)
    ring_y(1, 1)
    arrive(4, "core", steps=(0, 3, 1, 2))
    add_d_hidden(2)
    ring_y(0, 3)
    make_d()
    ring_y(1, 2)
    compute_dx(4)
    ring_x(0)
    compute_dx(3)
    ring_x(1)
    ring_y(1, 3)
    all_y(2)
    ring_y(2, 0)
    compute_dx(2)
    ring_x(2)
    ring_y(2, 1)
    end_y(0)
    compute_dx(1)
    ring_x(3)
    ring_y(2, 2)
    end_y(1)
    compute_dx(0)
    ring_y(2, 3)
    end_x()
    end_y(2)
    out_ref[0] = dot(y_rows[...], perm[...], NT).astype(jnp.bfloat16)

    for pair in range(len(PAIRS)):
        for i in range(2):
            for kind in PAIRS[pair][3]:
                copy(leg(pair, i, kind)[0], partner, pair, i, kind).wait_send()
    for g in range(GROUPS):
        release(y_buffers, (g,), Y_PARTS)
    release(x_buffers, (), X_PARTS)


def shards(tokens, cotangent, w_gate, w_up, w_down, slot_token, slot_gate, block_expert):
    vmem = pl.BlockSpec(memory_space=pltpu.VMEM)
    smem = pl.BlockSpec(memory_space=pltpu.SMEM)
    hbm = pl.BlockSpec(memory_space=pl.ANY)
    wide = (2, TOK, F)
    low, full, dma = jnp.bfloat16, jnp.float32, pltpu.SemaphoreType.DMA
    y_ring = (GROUPS, 2, Y_PARTS, HOPS)
    x_ring = (2, X_PARTS, HOPS)
    out = pl.pallas_call(
        kernel,
        out_shape=jax.ShapeDtypeStruct((2, TOK, COLS), low),
        in_specs=[smem] + [hbm] * 7,
        out_specs=vmem,
        scratch_shapes=[
            pltpu.VMEM((1, 512), jnp.int32),
            pltpu.VMEM((1, 512), jnp.int32),
            pltpu.VMEM((TOK, D), low),
            pltpu.VMEM((TOK, D), low),
            pltpu.VMEM((3, 2, ROWS, F), full),
            pltpu.VMEM((6, 2, 2, 2, 2, NC, ROWS, F), low),
            pltpu.VMEM((COLS, COLS), low),
            pltpu.VMEM((GROUPS, TOK, GK), low),
            pltpu.VMEM((2, GROUPS, TOK, GK), low),
            pltpu.VMEM((2, TOK, 1), full),
            pltpu.VMEM((4, TOK, F), full),
            pltpu.VMEM(wide, full),
            pltpu.VMEM(wide, low),
            pltpu.VMEM(wide, low),
            pltpu.VMEM(wide, low),
            pltpu.VMEM((GROUPS, NZ, TOK, GCOLS), full),
            pltpu.VMEM((NZ, TOK, COLS), full),
            pltpu.VMEM((TOK, COLS), low),
            pltpu.VMEM(y_ring + (TOK // Y_PARTS, GCOLS), low),
            pltpu.VMEM(y_ring + (TOK // Y_PARTS, GCOLS), low),
            pltpu.VMEM(x_ring + (TOK // X_PARTS, COLS), low),
            pltpu.VMEM(x_ring + (TOK // X_PARTS, COLS), low),
            dma((COPIES,)),
            dma((COPIES,)),
            dma(y_ring),
            dma(y_ring),
            dma(x_ring),
            dma(x_ring),
            dma((9,)),
        ],
        compiler_params=pltpu.CompilerParams(
            collective_id=0, has_side_effects=True, vmem_limit_bytes=63 * 1024 * 1024
        ),
    )(
        block_expert,
        slot_token.reshape(1, -1),
        slot_gate.reshape(1, -1),
        tokens,
        cotangent,
        w_gate,
        w_up,
        jnp.swapaxes(w_down, 1, 2),
    )
    return out[0], out[1]


def solution(mesh):
    in_specs = (
        P("dp", None),
        P("dp", None),
        P(None, "dp", "etp"),
        P(None, "dp", "etp"),
        P(None, "etp", "dp"),
        P("dp"),
        P("dp"),
        P("dp"),
    )
    out_specs = (P("dp", "etp"), P("dp", "etp"))
    return jax.shard_map(shards, mesh=mesh, in_specs=in_specs, out_specs=out_specs, check_vma=False)
```

time: 491 us -> 126 us (0.26)
  waiting for transfers between devices: 426 us -> 0 us
  Pallas kernels: 0 us -> 122 us
  local copies, waits for them, and re-layouts: 39.6 us -> 1.8 us
  between operations: 13.8 us -> 0.64 us
  other arithmetic: 6.36 us -> 0 us
    unnamed x7 -> x0, waiting for transfers between devices: 265 us -> none
    all_gather x3 -> x0, waiting for transfers between devices: 162 us -> none  [the longest x1 62.5 us: shards(): lax.all_gather(up_low, 'dp', axis=1, tiled=True)]
    pallas_call x0 -> x1, Pallas kernels: none -> 122 us  [shards(): pl.pallas_call(kernel, out_shape=jax.ShapeDtypeStruct((2, TOK, COLS), low...]
    while x1 -> x0, local copies, waits for them, and re-layouts: 23.8 us -> none  [shards(): totals = lax.fori_loop(0, block_count, visit_all, totals)]
    unnamed x11 -> x0, local copies, waits for them, and re-layouts: 11.1 us -> none
    convert_element_type x4 -> x0, other arithmetic: 6.36 us -> none  [the longest x1 1.81 us: shards(): gate_low = w_gate.astype(jnp.bfloat16)]
  transfers between devices with their start and end apart: 5 -> 0, of which waited for: 5 -> 0; matrix products, arithmetic and copies ran while one was open for 7% -> 0% of each run, Pallas kernels for 0% -> 0%
where the time goes in v3:
time: 126 us; the launch traced here: 124 us
  Pallas kernels  122 us (97%)
  local copies, waits for them, and re-layouts  1.8 us (1%)
    pallas_call x1, Pallas kernels, shards(): pl.pallas_call(kernel, out_shape=jax.ShapeDtypeStruct((2, TOK, COLS), low...  122 us

profile of v3, /device:TPU:4, one launch (start us, length us, event | category | flops | bytes accessed | tf_op | source)
XLA Modules:
  0.0 124.2 jit_solution(11478661343239808327)
XLA Ops:
  0.6 121.7 %shard_map.95 = bf16[2,256,384]{2,1,0:T(8,128)(2,1)} custom-call(s32[4]{0:T(128)} %expert_ref.1, s32[1,512]{1,0:T(1,128)} %bitcast.8, s32[1,512]{1,0:T(1,128)} %bitcast.9, bf16[256,3072]{1,0:T(8,128)(2,1)} %tokens_hbm.1, bf16[256,3072]{1,0:T(8,128)(2,1)} %cotangent_hbm.1, f32[2,96,768]{2,1,0:T(8,128)} %w_gate_hbm.1, f32[2,96,768]{2,1,0:T(8,128)} %w_up_hbm.1, ...), custom_call_target="tpu_custom_call" | custom-call | tf_op jit(solution)/shard_map/pallas_call | solution.py:516
  122.4 1.8 %slice_bitcast_fusion = (bf16[256,384]{1,0:T(8,128)(2,1)}, bf16[256,384]{1,0:T(8,128)(2,1)}) fusion(bf16[2,256,384]{2,1,0:T(8,128)(2,1)} %shard_map.95), kind=kLoop, calls=%fused_computation | loop fusion | bytes 786432 | tf_op jit(solution)/shard_map/squeeze | solution.py:565

commit v4 on v3

--- a/solution.py
+++ b/solution.py
@@ -225,16 +225,19 @@
             hidden[e, rows, :] = h.astype(jnp.bfloat16)
 
     def make_d():
-        @pl.loop(0, 2 * (TOK // 32))
+        g = GROUPS - 1
+
+        @pl.loop(0, 2 * (F // 256))
         def _(j):
-            e = j // (TOK // 32)
-            rows = pl.ds(pl.multiple_of((j % (TOK // 32)) * 32, 32), 32)
-            gate = pre[2 * e, rows, :]
-            dh = d_hidden[e, rows, :]
+            e = j // (F // 256)
+            cols = pl.ds(pl.multiple_of((j % (F // 256)) * 256, 256), 256)
+            rhs = w_all[4 + e, :, :, :, :, :, pl.ds(g * GROUP, GROUP), cols].reshape(GK, 256)
+            dh = d_hidden[e, :, cols] + dot(d_out[e, g], rhs, NN)
+            gate = pre[2 * e, :, cols]
             squash = 1.0 / (1.0 + jnp.exp(-gate))
-            before = dh * pre[2 * e + 1, rows, :] * squash * (1.0 + gate * (1.0 - squash))
-            d_pre[e, rows, :] = before.astype(jnp.bfloat16)
-            d_up[e, rows, :] = (dh * (gate * squash)).astype(jnp.bfloat16)
+            before = dh * pre[2 * e + 1, :, cols] * squash * (1.0 + gate * (1.0 - squash))
+            d_pre[e, :, cols] = before.astype(jnp.bfloat16)
+            d_up[e, :, cols] = (dh * (gate * squash)).astype(jnp.bfloat16)
 
     loads[0].wait()
     cast(0, GATE, 0)
@@ -310,9 +313,10 @@
 
     loads[8].wait()
 
-    def all_y(g):
-        @pl.loop(0, NX)
-        def _(n):
+    def some_y(g, first, last):
+        @pl.loop(first, last)
+        def _(j):
+            n = lax.rem((z + HOPS) // 2 + j, NX)
             total = 0.0
             for e in range(2):
                 rows = w_all[4 + e, n // 2, n % 2, :, :, :, pl.ds(g * GROUP, GROUP), :]
@@ -453,48 +457,47 @@
     arrive(2, "turn2")
     start(2, "core", steps=(2,))
     arrive(2, "core", steps=(0, 3, 1, 2))
-    all_y(0)
+    some_y(0, 0, NX)
     ring_y(0, 0)
+    add_d_hidden(0)
     arrive(4, "turn")
     start(4, "turn2")
     start(4, "core", steps=(3, 1))
-    add_d_hidden(0)
     ring_y(0, 1)
     arrive(3, "turn2")
     start(3, "core", steps=(2,))
     arrive(3, "core", steps=(0, 3, 1, 2))
-    all_y(1)
+    some_y(1, 0, NX)
     ring_y(1, 0)
+    ring_y(0, 2)
     arrive(4, "turn2")
     start(4, "core", steps=(2,))
-    ring_y(0, 2)
     add_d_hidden(1)
     ring_y(1, 1)
     arrive(4, "core", steps=(0, 3, 1, 2))
-    add_d_hidden(2)
+    some_y(2, 0, 1)
+    ring_y(2, 0)
     ring_y(0, 3)
     make_d()
     ring_y(1, 2)
     compute_dx(4)
     ring_x(0)
+    some_y(2, 1, NX)
+    ring_y(2, 1)
     compute_dx(3)
     ring_x(1)
     ring_y(1, 3)
-    all_y(2)
-    ring_y(2, 0)
+    ring_y(2, 2)
     compute_dx(2)
     ring_x(2)
-    ring_y(2, 1)
-    end_y(0)
+    ring_y(2, 3)
     compute_dx(1)
     ring_x(3)
-    ring_y(2, 2)
-    end_y(1)
     compute_dx(0)
-    ring_y(2, 3)
+    for g in range(GROUPS):
+        end_y(g)
+    out_ref[0] = dot(y_rows[...], perm[...], NT).astype(jnp.bfloat16)
     end_x()
-    end_y(2)
-    out_ref[0] = dot(y_rows[...], perm[...], NT).astype(jnp.bfloat16)
 
     for pair in range(len(PAIRS)):
         for i in range(2):

time: 126 us -> 122 us (0.968)
  Pallas kernels: 122 us -> 118 us
    pallas_call x1, Pallas kernels: 122 us -> 118 us  [shards(): pl.pallas_call(kernel, out_shape=jax.ShapeDtypeStruct((2, TOK, COLS), low...]
where the time goes in v4:
time: 122 us; the launch traced here: 121 us
  Pallas kernels  118 us (97%)
  local copies, waits for them, and re-layouts  1.8 us (1%)
    pallas_call x1, Pallas kernels, shards(): pl.pallas_call(kernel, out_shape=jax.ShapeDtypeStruct((2, TOK, COLS), low...  118 us

profile of v4, /device:TPU:4, one launch (start us, length us, event | category | flops | bytes accessed | tf_op | source)
XLA Modules:
  0.0 120.9 jit_solution(9702065429349302025)
XLA Ops:
  0.6 118.4 %shard_map.95 = bf16[2,256,384]{2,1,0:T(8,128)(2,1)} custom-call(s32[4]{0:T(128)} %expert_ref.1, s32[1,512]{1,0:T(1,128)} %bitcast.8, s32[1,512]{1,0:T(1,128)} %bitcast.9, bf16[256,3072]{1,0:T(8,128)(2,1)} %tokens_hbm.1, bf16[256,3072]{1,0:T(8,128)(2,1)} %cotangent_hbm.1, f32[2,96,768]{2,1,0:T(8,128)} %w_gate_hbm.1, f32[2,96,768]{2,1,0:T(8,128)} %w_up_hbm.1, ...), custom_call_target="tpu_custom_call" | custom-call | tf_op jit(solution)/shard_map/pallas_call | solution.py:519
  119.1 1.8 %slice_bitcast_fusion = (bf16[256,384]{1,0:T(8,128)(2,1)}, bf16[256,384]{1,0:T(8,128)(2,1)}) fusion(bf16[2,256,384]{2,1,0:T(8,128)(2,1)} %shard_map.95), kind=kLoop, calls=%fused_computation | loop fusion | bytes 786432 | tf_op jit(solution)/shard_map/squeeze | solution.py:568

commit v5 on v4

--- a/solution.py
+++ b/solution.py
@@ -58,6 +58,7 @@
     w_gate_hbm,
     w_up_hbm,
     w_down_hbm,
+    out_hbm,
     out_ref,
     slot_token_ref,
     slot_gate_ref,
@@ -88,6 +89,7 @@
     xs_sem,
     xr_sem,
     l_sem,
+    o_sem,
 ):
     dp = lax.axis_index("dp")
     z = lax.axis_index("etp")
@@ -125,7 +127,9 @@
         (tokens_hbm, tokens_ref),
     ):
         loads.append(pltpu.make_async_copy(src, dst, l_sem.at[len(loads)]))
-        loads[-1].start()
+
+    for load in loads[:5]:
+        load.start()
 
     def cast(m, name, e):
         w_all[name[e], x // 2, x % 2, y // 2, y % 2, c, :, :] = masters[m, e].astype(jnp.bfloat16)
@@ -196,6 +200,11 @@
             for i in range(2):
                 copy(leg(pair, i, (name, part, step))[2], partner, pair, i, (name, part, step)).wait_recv()
 
+    def retire(pair):
+        for i in range(2):
+            for kind in PAIRS[pair][3]:
+                copy(leg(pair, i, kind)[0], partner, pair, i, kind).wait_send()
+
     def forward(first):
         @pl.loop(0, 2 * (F // 256))
         def _(j):
@@ -246,6 +255,8 @@
     barrier_wait()
     start(0, "near")
     start(0, "turn", OWN)
+    for load in loads[5:]:
+        load.start()
     loads[2].wait()
     cast(0, GATE, 1)
     loads[3].wait()
@@ -392,12 +403,19 @@
     def ring_x(step):
         ring(x_buffers, part_x, (), X_PARTS, step)
 
+    def store(t, h, size):
+        rows = pl.ds(h * size, size)
+        return pltpu.make_async_copy(out_ref.at[t, rows], out_hbm.at[t, rows], o_sem.at[t, h])
+
     def end_x():
         size = TOK // X_PARTS
         for n in range(X_PARTS):
             h = n // 2 + (n % 2) * (X_PARTS // 2)
             rows = collect(x_buffers, part_x, (), X_PARTS, h)
             out_ref[1, h * size : (h + 1) * size, :] = rows
+            store(1, h, size).start()
+        for h in range(X_PARTS):
+            store(1, h, size).wait()
 
     def weight_block(p, b):
         rows = w_all[p, b // 4, (b // 2) % 2, b % 2, :, :, :, :]
@@ -464,6 +482,7 @@
     start(4, "turn2")
     start(4, "core", steps=(3, 1))
     ring_y(0, 1)
+    retire(0)
     arrive(3, "turn2")
     start(3, "core", steps=(2,))
     arrive(3, "core", steps=(0, 3, 1, 2))
@@ -494,22 +513,20 @@
     compute_dx(1)
     ring_x(3)
     compute_dx(0)
+    for pair in range(1, len(PAIRS)):
+        retire(pair)
     for g in range(GROUPS):
         end_y(g)
+        release(y_buffers, (g,), Y_PARTS)
     out_ref[0] = dot(y_rows[...], perm[...], NT).astype(jnp.bfloat16)
+    store(0, 0, TOK).start()
     end_x()
-
-    for pair in range(len(PAIRS)):
-        for i in range(2):
-            for kind in PAIRS[pair][3]:
-                copy(leg(pair, i, kind)[0], partner, pair, i, kind).wait_send()
-    for g in range(GROUPS):
-        release(y_buffers, (g,), Y_PARTS)
+    store(0, 0, TOK).wait()
+
     release(x_buffers, (), X_PARTS)
 
 
 def shards(tokens, cotangent, w_gate, w_up, w_down, slot_token, slot_gate, block_expert):
-    vmem = pl.BlockSpec(memory_space=pltpu.VMEM)
     smem = pl.BlockSpec(memory_space=pltpu.SMEM)
     hbm = pl.BlockSpec(memory_space=pl.ANY)
     wide = (2, TOK, F)
@@ -520,8 +537,9 @@
         kernel,
         out_shape=jax.ShapeDtypeStruct((2, TOK, COLS), low),
         in_specs=[smem] + [hbm] * 7,
-        out_specs=vmem,
+        out_specs=hbm,
         scratch_shapes=[
+            pltpu.VMEM((2, TOK, COLS), low),
             pltpu.VMEM((1, 512), jnp.int32),
             pltpu.VMEM((1, 512), jnp.int32),
             pltpu.VMEM((TOK, D), low),
@@ -551,6 +569,7 @@
             dma(x_ring),
             dma(x_ring),
             dma((9,)),
+            dma((2, X_PARTS)),
         ],
         compiler_params=pltpu.CompilerParams(
             collective_id=0, has_side_effects=True, vmem_limit_bytes=63 * 1024 * 1024

time: 122 us -> 121 us (level)
  no operation moved by 1% of the time
where the time goes in v5:
time: 121 us
  Pallas kernels  118 us (98%)
  local copies, waits for them, and re-layouts  1.8 us (1%)
    pallas_call x1, Pallas kernels, shards(): pl.pallas_call(kernel, out_shape=jax.ShapeDtypeStruct((2, TOK, COLS), low...  118 us

profile of v5, /device:TPU:4, one launch (start us, length us, event | category | flops | bytes accessed | tf_op | source)
XLA Modules:
  0.0 120.5 jit_solution(14842833820414984471)
XLA Ops:
  0.6 118.1 %shard_map.95 = bf16[2,256,384]{2,1,0:T(8,128)(2,1)} custom-call(s32[4]{0:T(128)} %expert_ref.1, s32[1,512]{1,0:T(1,128)} %bitcast.8, s32[1,512]{1,0:T(1,128)} %bitcast.9, bf16[256,3072]{1,0:T(8,128)(2,1)} %tokens_hbm.1, bf16[256,3072]{1,0:T(8,128)(2,1)} %cotangent_hbm.1, f32[2,96,768]{2,1,0:T(8,128)} %w_gate_hbm.1, f32[2,96,768]{2,1,0:T(8,128)} %w_up_hbm.1, ...), custom_call_target="tpu_custom_call" | custom-call | tf_op jit(solution)/shard_map/pallas_call | solution.py:536
  118.7 1.8 %slice_bitcast_fusion = (bf16[256,384]{1,0:T(8,128)(2,1)}, bf16[256,384]{1,0:T(8,128)(2,1)}) fusion(bf16[2,256,384]{2,1,0:T(8,128)(2,1)} %shard_map.95), kind=kLoop, calls=%fused_computation | loop fusion | bytes 786432 | tf_op jit(solution)/shard_map/squeeze | solution.py:587

commit v6 on v5

--- a/solution.py
+++ b/solution.py
@@ -189,9 +189,9 @@
             device_id_type=MESH,
         )
 
-    def start(pair, name, part=ALL, steps=(1, 3)):
+    def start(pair, name, part=ALL, steps=(1, 3), which=(0, 1)):
         for step in steps:
-            for i in range(2):
+            for i in which:
                 ref, peer, _ = leg(pair, i, (name, part, step))
                 copy(ref, peer, pair, i, (name, part, step)).start()
 
@@ -250,11 +250,13 @@
 
     loads[0].wait()
     cast(0, GATE, 0)
+    barrier_wait()
+    start(0, "near", which=(0,))
+    start(0, "turn", OWN, which=(0,))
     loads[1].wait()
     cast(1, UP, 0)
-    barrier_wait()
-    start(0, "near")
-    start(0, "turn", OWN)
+    start(0, "near", which=(1,))
+    start(0, "turn", OWN, which=(1,))
     for load in loads[5:]:
         load.start()
     loads[2].wait()

time: 121 us -> 121 us (level)
  no operation moved by 1% of the time
where the time goes in v6:
time: 121 us
  Pallas kernels  118 us (98%)
  local copies, waits for them, and re-layouts  1.8 us (1%)
    pallas_call x1, Pallas kernels, shards(): pl.pallas_call(kernel, out_shape=jax.ShapeDtypeStruct((2, TOK, COLS), low...  118 us

profile of v6, /device:TPU:4, one launch (start us, length us, event | category | flops | bytes accessed | tf_op | source)
XLA Modules:
  0.0 120.5 jit_solution(10598597425256644641)
XLA Ops:
  0.6 118.1 %shard_map.95 = bf16[2,256,384]{2,1,0:T(8,128)(2,1)} custom-call(s32[4]{0:T(128)} %expert_ref.1, s32[1,512]{1,0:T(1,128)} %bitcast.8, s32[1,512]{1,0:T(1,128)} %bitcast.9, bf16[256,3072]{1,0:T(8,128)(2,1)} %tokens_hbm.1, bf16[256,3072]{1,0:T(8,128)(2,1)} %cotangent_hbm.1, f32[2,96,768]{2,1,0:T(8,128)} %w_gate_hbm.1, f32[2,96,768]{2,1,0:T(8,128)} %w_up_hbm.1, ...), custom_call_target="tpu_custom_call" | custom-call | tf_op jit(solution)/shard_map/pallas_call | solution.py:538
  118.7 1.8 %slice_bitcast_fusion = (bf16[256,384]{1,0:T(8,128)(2,1)}, bf16[256,384]{1,0:T(8,128)(2,1)}) fusion(bf16[2,256,384]{2,1,0:T(8,128)(2,1)} %shard_map.95), kind=kLoop, calls=%fused_computation | loop fusion | bytes 786432 | tf_op jit(solution)/shard_map/squeeze | solution.py:589
